TPU v7x, 512 devices: a whole 4x4x16 slice. The times are simulated.
512 devices in a mesh: seq: 128 (over z, y, core), mp: 4 (over x).
Axes of the slice: x: 4, y: 4, z: 16, core: 2. Of those that a mesh axis runs over, the one named last changes fastest.
Arguments:
- queries: bfloat16 [8192, 2048], P('seq', 'mp'), may hold values from -14 to 14
- keys: bfloat16 [8192, 2048], P('seq', 'mp'), may hold values from -14 to 14
- values: bfloat16 [8192, 2048], P('seq', 'mp'), may hold values from -6 to 6
- stream: bfloat16 [8192, 2048], P('seq', 'mp'), may hold values from -6 to 6
- seg_lengths: int32 [64], replicated, may hold values from 1 to 256, 8192 in all
- gain: float32 [2048], replicated, may hold values from 0.5 to 1.5
- w_out: bfloat16 [2048, 2048], P('mp', 'seq'), may hold values from -0.125 to 0.125
- w_gate: bfloat16 [2048, 3072], P('seq', 'mp'), may hold values from -0.125 to 0.125
- w_up: bfloat16 [2048, 3072], P('seq', 'mp'), may hold values from -0.125 to 0.125
- w_down: bfloat16 [3072, 2048], P('mp', 'seq'), may hold values from -0.109375 to 0.109375
Outputs:
- mixed: bfloat16 [8192, 2048], P('seq', 'mp')
Inputs may be any that keep to these rules, and one draw needn't show every extreme that they name: `seg_lengths`: the segments of landmarks 0 to 63 follow one another and cover the document's 8192 tokens.
All inputs are finite; a program needn't handle non-finite values.
Results may differ from a plain program's by a relative error of at most 0.014.
Values may be sent and summed in bfloat16 or wider, within the bound.
No kernel may reach another device: no remote copies, remote signals or barrier semaphores. Data moves between devices by JAX's collectives and lax.ppermute only.
A program may use at most 64 MiB of HBM per device.

v0:
```python
import math

import jax
import jax.numpy as jnp
from jax import lax
from jax.sharding import PartitionSpec as P

PINV_ITERS = 6
HEAD = 128


HIGH_ACCURACY = lax.Precision.HIGHEST
EPS = 1e-05


def inverse_rounds(anchor_block):
    eye = jnp.eye(anchor_block.shape[-1], dtype=jnp.float32)
    col_most = jnp.max(jnp.sum(anchor_block, axis=1), axis=-1)
    row_most = jnp.max(jnp.sum(anchor_block, axis=2), axis=-1)
    approx = jnp.swapaxes(anchor_block, 1, 2) / (col_most * row_most)[:, None, None]
    for step in range(PINV_ITERS):
        prod = jnp.einsum("hij,hjk->hik", anchor_block, approx, precision=HIGH_ACCURACY)
        inner = 7.0 * eye - prod
        inner = 15.0 * eye - jnp.einsum("hij,hjk->hik", prod, inner, precision=HIGH_ACCURACY)
        inner = 13.0 * eye - jnp.einsum("hij,hjk->hik", prod, inner, precision=HIGH_ACCURACY)
        approx = 0.25 * jnp.einsum("hij,hjk->hik", approx, inner, precision=HIGH_ACCURACY)
    return approx


def on_device(queries, keys, values, stream, seg_lengths, gain, w_out, w_gate, w_up, w_down):
    tok = queries.shape[0]
    width = queries.shape[1]
    heads = width // HEAD
    marks = seg_lengths.shape[0]
    score_scale = 1.0 / math.sqrt(HEAD)
    ends = jnp.cumsum(seg_lengths)
    starts = ends - seg_lengths
    place = lax.axis_index("seq") * tok + jnp.arange(tok, dtype=jnp.int32)
    member = ((place[:, None] >= starts[None, :]) & (place[:, None] < ends[None, :])).astype(
        jnp.bfloat16
    )
    query_part = jnp.dot(member.T, queries, preferred_element_type=jnp.float32)
    key_part = jnp.dot(member.T, keys, preferred_element_type=jnp.float32)
    query_sum, key_sum = lax.psum((query_part, key_part), "seq")
    counts = seg_lengths.astype(jnp.float32)[:, None]
    query_anchors = (query_sum / counts).reshape(marks, heads, HEAD)
    key_anchors = (key_sum / counts).reshape(marks, heads, HEAD)
    query_slice = queries.astype(jnp.float32).reshape(tok, heads, HEAD)
    key_slice = keys.astype(jnp.float32).reshape(tok, heads, HEAD)
    value_slice = values.astype(jnp.float32).reshape(tok, heads, HEAD)
    nearby_scores = jax.nn.softmax(
        jnp.einsum("brc,xrc->rbx", query_slice, key_anchors, precision=HIGH_ACCURACY) * score_scale,
        axis=-1,
    )
    anchor_block = jax.nn.softmax(
        jnp.einsum("oqc,bqc->qob", query_anchors, key_anchors, precision=HIGH_ACCURACY)
        * score_scale,
        axis=-1,
    )
    distant_scores = (
        jnp.einsum("gvb,lvb->vgl", query_anchors, key_slice, precision=HIGH_ACCURACY) * score_scale
    )
    local_peak = jnp.max(distant_scores, axis=-1)
    peak = lax.pmax(local_peak, "seq")
    layer_weights = jnp.exp(distant_scores - peak[..., None])
    local_mass = jnp.sum(layer_weights, axis=-1)
    slice_sum = jnp.einsum("vqb,bvn->vqn", layer_weights, value_slice, precision=HIGH_ACCURACY)
    mass, weighted = lax.psum((local_mass, slice_sum), "seq")
    collected_rows = weighted / mass[..., None]
    token_mixer = jnp.einsum(
        "svy,syc->svc", inverse_rounds(anchor_block), collected_rows, precision=HIGH_ACCURACY
    )
    attn = (
        jnp.einsum("ljz,lzx->jlx", nearby_scores, token_mixer, precision=HIGH_ACCURACY)
        .reshape(tok, width)
        .astype(jnp.bfloat16)
    )
    full_out = lax.all_gather(w_out, "seq", axis=1, tiled=True)
    out_terms = jnp.dot(attn, full_out, preferred_element_type=jnp.float32)
    proj = lax.psum_scatter(
        out_terms.astype(jnp.bfloat16), "mp", scatter_dimension=1, tiled=True
    ).astype(jnp.float32)
    resid = (stream.astype(jnp.float32) + proj).astype(jnp.bfloat16)
    whole = lax.all_gather(resid, "mp", axis=1, tiled=True)
    whole32 = whole.astype(jnp.float32)
    meansq = jnp.mean(whole32 * whole32, axis=-1, keepdims=True)
    normed = (whole32 * lax.rsqrt(meansq + EPS) * gain[None, :]).astype(jnp.bfloat16)
    full_gate, full_up = (
        lax.all_gather(w_gate, "seq", axis=0, tiled=True),
        lax.all_gather(w_up, "seq", axis=0, tiled=True),
    )
    gate = jnp.dot(normed, full_gate, preferred_element_type=jnp.float32)
    upper = jnp.dot(normed, full_up, preferred_element_type=jnp.float32)
    hidden = (jax.nn.silu(gate) * upper).astype(jnp.bfloat16)
    full_down = lax.all_gather(w_down, "seq", axis=1, tiled=True)
    down_terms = jnp.dot(hidden, full_down, preferred_element_type=jnp.float32)
    ffn = lax.psum_scatter(
        down_terms.astype(jnp.bfloat16), "mp", scatter_dimension=1, tiled=True
    ).astype(jnp.float32)
    return (resid.astype(jnp.float32) + ffn).astype(jnp.bfloat16)


def solution(mesh):
    return jax.shard_map(
        on_device,
        mesh=mesh,
        in_specs=(
            P("seq", "mp"),
            P("seq", "mp"),
            P("seq", "mp"),
            P("seq", "mp"),
            P(),
            P(),
            P("mp", "seq"),
            P("seq", "mp"),
            P("seq", "mp"),
            P("mp", "seq"),
        ),
        out_specs=P("seq", "mp"),
        check_vma=False,
    )
```

profile of v0, /device:TPU:24, one launch (start us, length us, event | category | flops | bytes accessed | tf_op | source)
XLA Modules:
  0.0 1538.8 jit_solution(13063598890913038582)
XLA Ops:
  6.5 0.8 copy.40
  7.3 0.1 reduce-window.8
  7.4 0.1 reduce
  7.5 0.7 fusion.82
  8.3 1.8 fusion.60
  10.1 0.0 all-reduce.6.cloned.1.call-start
  10.1 0.9 fusion.59
  11.0 322.6 %all-reduce.4.cloned.1.call-done = f32[64,512]{1,0:T(8,128)} async-done(((f32[64,512]{1,0:T(8,128)}), f32[64,512]{1,0:T(8,128)}) %all-reduce.4.cloned.1.call-update) | async-done | bytes 131088 | tf_op jit(solution)/shard_map/psum | solution.py:44
  333.6 1.2 fusion.83
  334.9 234.4 %pmax.7 = f32[4,64]{1,0:T(4,128)S(1)} all-reduce(f32[4,64]{1,0:T(4,128)S(1)} %get-tuple-element.11), channel_id=1, replica_groups=mesh['seq'=128,'mp'=4] {'seq'}, use_global_device_ids=true, to_apply=%region_10.11 | all-reduce | flops 256 | bytes 2048 | tf_op jit(solution)/shard_map/pmax | solution.py:64
  569.2 1.8 fusion.29
  571.0 0.0 all-gather.5.cloned.1.call-start
  571.1 0.7 all-gather.5.cloned.1.call-update
  571.9 246.9 %psum.31 = f32[4,64]{1,0:T(4,128)S(1)} all-reduce(f32[4,64]{1,0:T(4,128)S(1)} %fusion.28), channel_id=1, replica_groups=mesh['seq'=128,'mp'=4] {'seq'}, use_global_device_ids=true, to_apply=%region_13.14 | all-reduce | flops 256 | bytes 2048 | tf_op jit(solution)/shard_map/psum | solution.py:68
  818.8 87.1 %all-reduce.6.cloned.1.call-done = (f32[64,512]{1,0:T(8,128)}, f32[4,64,128]{2,1,0:T(8,128)}) async-done(((f32[64,512]{1,0:T(8,128)}, f32[4,64,128]{2,1,0:T(8,128)}), (f32[64,512]{1,0:T(8,128)}, f32[4,64,128]{2,1,0:T(8,128)})) %all-reduce.6.cloned.1.call-update) | async-done | bytes 262160 | tf_op jit(solution)/shard_map/psum | solution.py:44
  905.9 1.3 fusion.85
  907.2 1.4 fusion.84
  908.7 0.1 fusion.80
  908.8 0.1 reduce_max.46
  908.9 0.1 reduce_max.47
  909.1 0.4 fusion.68
  909.5 0.3 convolution_subtract_fusion.11
  909.8 0.3 convolution_subtract_fusion.10
  910.0 0.3 convolution_multiply_fusion.8
  910.4 0.4 fusion.77
  910.8 0.3 convolution_subtract_fusion.9
  911.0 0.3 convolution_subtract_fusion.8
  911.3 0.3 convolution_multiply_fusion.7
  911.6 0.2 fusion.30
  911.8 0.4 fusion.75
  912.2 0.3 convolution_subtract_fusion.7
  912.4 0.3 convolution_subtract_fusion.6
  912.7 0.3 convolution_multiply_fusion.6
  913.0 0.4 fusion.73
  913.4 0.3 convolution_subtract_fusion.5
  913.6 0.3 convolution_subtract_fusion.4
  913.9 0.3 convolution_multiply_fusion.5
  914.2 0.4 fusion.71
  914.6 0.3 convolution_subtract_fusion.3
  914.8 0.3 convolution_subtract_fusion.2
  915.1 0.3 convolution_multiply_fusion.4
  915.4 0.4 fusion.69
  915.8 0.3 convolution_subtract_fusion.1
  916.1 0.3 convolution_subtract_fusion
  916.3 0.3 convolution_multiply_fusion.3
  916.6 0.4 fusion.22
  917.0 0.4 fusion.2
  917.3 128.4 %all-gather.5.cloned.1.call-done = bf16[512,2048]{0,1:T(8,128)(2,1)} async-done(((bf16[512,16]{0,1:T(8,128)(2,1)}), bf16[512,2048]{0,1:T(8,128)(2,1)}) %all-gather.5.cloned.1.call-update) | async-done | bytes 2097168 | tf_op jit(solution)/shard_map/all_gather | solution.py:78
  1045.7 3.0 convolution_convert_fusion.1
  1048.8 0.0 all-gather.7.cloned.1.call-start
  1048.9 0.5 all-gather.7.cloned.1.call-update
  1049.5 0.5 all-gather.11.cloned.1.call-update
  1050.0 0.7 all-gather.9.cloned.1.call-update
  1050.8 23.7 %reduce-scatter.3.cloned.1.call-done = bf16[64,512]{1,0:T(8,128)(2,1)} async-done(((bf16[64,2048]{1,0:T(8,128)(2,1)}), bf16[64,512]{1,0:T(8,128)(2,1)}) %reduce-scatter.3.cloned.1.call-update) | async-done | bytes 65552 | tf_op jit(solution)/shard_map/reduce_scatter | solution.py:80
  1074.5 0.9 add_convert_fusion.1
  1075.3 12.3 all_gather.16
  1087.6 0.2 fusion.3
  1087.7 130.0 %all-gather.7.cloned.1.call-done = bf16[2048,768]{1,0:T(8,128)(2,1)} async-done(((bf16[16,768]{1,0:T(8,128)(2,1)}), bf16[2048,768]{1,0:T(8,128)(2,1)}) %all-gather.7.cloned.1.call-update) | async-done | bytes 3145744 | tf_op jit(solution)/shard_map/all_gather | solution.py:89
  1217.8 2.6 fusion.36
  1220.4 138.2 %all-gather.11.cloned.1.call-done = bf16[768,2048]{0,1:T(8,128)(2,1)} async-done(((bf16[768,16]{0,1:T(8,128)(2,1)}), bf16[768,2048]{0,1:T(8,128)(2,1)}) %all-gather.11.cloned.1.call-update) | async-done | bytes 3145744 | tf_op jit(solution)/shard_map/all_gather | solution.py:95
  1358.5 140.8 %all-gather.9.cloned.1.call-done = bf16[2048,768]{1,0:T(8,128)(2,1)} async-done(((bf16[16,768]{1,0:T(8,128)(2,1)}), bf16[2048,768]{1,0:T(8,128)(2,1)}) %all-gather.9.cloned.1.call-update) | async-done | bytes 3145744 | tf_op jit(solution)/shard_map/all_gather | solution.py:90
  1499.4 5.3 convolution_convert_fusion
  1504.7 25.7 %reduce-scatter.5.cloned.1.call-done = bf16[64,512]{1,0:T(8,128)(2,1)} async-done(((bf16[64,2048]{1,0:T(8,128)(2,1)}), bf16[64,512]{1,0:T(8,128)(2,1)}) %reduce-scatter.5.cloned.1.call-update) | async-done | bytes 65552 | tf_op jit(solution)/shard_map/reduce_scatter | solution.py:97
  1530.5 1.5 add_convert_fusion
  (23 shorter events, 0.4 us)
Async XLA Ops:
  6.5 3.6 copy-start
  6.5 327.1 %all-reduce.4.cloned.1.call-start = ((), (), s32[]{:S(2)}) async-start(), calls=%async_computation.2 | async-start | bytes 262144 | tf_op jit(solution)/shard_map/psum | solution.py:44
  10.1 895.9 %all-reduce.6.cloned.1.call-start = ((), (), s32[]{:S(2)}) async-start(), calls=%async_computation.9 | async-start | bytes 524288 | tf_op jit(solution)/shard_map/psum | solution.py:44
  571.0 474.7 %all-gather.5.cloned.1.call-start = ((), (), s32[]{:S(2)}) async-start(), calls=%async_computation.3 | async-start | bytes 2113536 | tf_op jit(solution)/shard_map/all_gather | solution.py:78
  571.8 502.7 %reduce-scatter.3.cloned.1.call-start = ((), (), s32[]{:S(2)}) async-start(), calls=%async_computation.4 | async-start | bytes 327680 | tf_op jit(solution)/shard_map/reduce_scatter | solution.py:80
  912.4 4.2 copy-start.3
  914.8 159.6 %copy-start.1 = (bf16[64,512]{1,0:T(8,128)(2,1)S(1)}, bf16[64,512]{1,0:T(8,128)(2,1)}, u32[]{:S(2)}) copy-start(bf16[64,512]{1,0:T(8,128)(2,1)} %param.13) | copy-start | bytes 196612
  915.4 302.4 %copy-start.2 = (f32[2048]{0:T(1024)S(1)}, f32[2048]{0:T(1024)}, u32[]{:S(2)}) copy-start(f32[2048]{0:T(1024)} %param.15) | copy-start | bytes 24580
  1048.8 168.9 %all-gather.7.cloned.1.call-start = ((), (), s32[]{:S(2)}) async-start(), calls=%async_computation.5 | async-start | bytes 3170304 | tf_op jit(solution)/shard_map/all_gather | solution.py:89
  1049.4 309.1 %all-gather.11.cloned.1.call-start = ((), (), s32[]{:S(2)}) async-start(), calls=%async_computation.7 | async-start | bytes 3170304 | tf_op jit(solution)/shard_map/all_gather | solution.py:95
  1050.0 449.4 %all-gather.9.cloned.1.call-start = ((), (), s32[]{:S(2)}) async-start(), calls=%async_computation.6 | async-start | bytes 3170304 | tf_op jit(solution)/shard_map/all_gather | solution.py:90
  1050.7 479.7 %reduce-scatter.5.cloned.1.call-start = ((), (), s32[]{:S(2)}) async-start(), calls=%async_computation.8 | async-start | bytes 327680 | tf_op jit(solution)/shard_map/reduce_scatter | solution.py:97
Sparse Core Ops, SparseCore 0:
  10.8 322.7 all-reduce.3
  571.1 334.7 all-reduce.5
  909.1 136.6 all-gather.4
  1048.9 25.4 reduce-scatter.2
  1077.9 139.8 all-gather.6
  1221.2 137.2 all-gather.10
  1362.1 137.2 all-gather.8
  1504.8 25.5 reduce-scatter.4
where the time goes:
time: 1540 us
  waiting for transfers between devices  999 us (65%)
  blocking collectives  494 us (32%)
  matrix products  27.2 us (2%)
    psum x2, waiting for transfers between devices, on_device(): query_sum, key_sum = lax.psum((query_part, key_part), 'seq')  410 us
    psum x1, blocking collectives, on_device(): mass, weighted = lax.psum((local_mass, slice_sum), 'seq')  247 us
    pmax x1, blocking collectives, on_device(): peak = lax.pmax(local_peak, 'seq')  234 us
    all_gather x1, waiting for transfers between devices, on_device(): lax.all_gather(w_up, 'seq', axis=0, tiled=True)  141 us
    all_gather x1, waiting for transfers between devices, on_device(): full_down = lax.all_gather(w_down, 'seq', axis=1, tiled=True)  138 us
    all_gather x1, waiting for transfers between devices, on_device(): lax.all_gather(w_gate, 'seq', axis=0, tiled=True)  130 us
    all_gather x1, waiting for transfers between devices, on_device(): full_out = lax.all_gather(w_out, 'seq', axis=1, tiled=True)  128 us
  transfers between devices with their start and end apart: 8, of which 8 were waited for; matrix products, arithmetic and copies ran while one was open for 1% of the time, Pallas kernels for 0%

commit v1 on v0

--- a/solution.py
+++ b/solution.py
@@ -3,7 +3,7 @@
 import jax
 import jax.numpy as jnp
 from jax import lax
-from jax.sharding import PartitionSpec as P
+from jax.sharding import Mesh, PartitionSpec as P
 
 PINV_ITERS = 6
 HEAD = 128
@@ -27,6 +27,34 @@
     return approx
 
 
+SEQ_AXES = ("z", "y", "c")
+
+
+def seq_psum(x):
+    for ax in reversed(SEQ_AXES):
+        x = lax.psum(x, ax)
+    return x
+
+
+def seq_pmax(x):
+    for ax in reversed(SEQ_AXES):
+        x = lax.pmax(x, ax)
+    return x
+
+
+def seq_gather(x, axis):
+    for ax in reversed(SEQ_AXES):
+        x = lax.all_gather(x, ax, axis=axis, tiled=True)
+    return x
+
+
+def seq_index():
+    idx = lax.axis_index(SEQ_AXES[0])
+    for ax in SEQ_AXES[1:]:
+        idx = idx * lax.axis_size(ax) + lax.axis_index(ax)
+    return idx
+
+
 def on_device(queries, keys, values, stream, seg_lengths, gain, w_out, w_gate, w_up, w_down):
     tok = queries.shape[0]
     width = queries.shape[1]
@@ -35,13 +63,13 @@
     score_scale = 1.0 / math.sqrt(HEAD)
     ends = jnp.cumsum(seg_lengths)
     starts = ends - seg_lengths
-    place = lax.axis_index("seq") * tok + jnp.arange(tok, dtype=jnp.int32)
+    place = seq_index() * tok + jnp.arange(tok, dtype=jnp.int32)
     member = ((place[:, None] >= starts[None, :]) & (place[:, None] < ends[None, :])).astype(
         jnp.bfloat16
     )
     query_part = jnp.dot(member.T, queries, preferred_element_type=jnp.float32)
     key_part = jnp.dot(member.T, keys, preferred_element_type=jnp.float32)
-    query_sum, key_sum = lax.psum((query_part, key_part), "seq")
+    query_sum, key_sum = seq_psum((query_part, key_part))
     counts = seg_lengths.astype(jnp.float32)[:, None]
     query_anchors = (query_sum / counts).reshape(marks, heads, HEAD)
     key_anchors = (key_sum / counts).reshape(marks, heads, HEAD)
@@ -61,11 +89,11 @@
         jnp.einsum("gvb,lvb->vgl", query_anchors, key_slice, precision=HIGH_ACCURACY) * score_scale
     )
     local_peak = jnp.max(distant_scores, axis=-1)
-    peak = lax.pmax(local_peak, "seq")
+    peak = seq_pmax(local_peak)
     layer_weights = jnp.exp(distant_scores - peak[..., None])
     local_mass = jnp.sum(layer_weights, axis=-1)
     slice_sum = jnp.einsum("vqb,bvn->vqn", layer_weights, value_slice, precision=HIGH_ACCURACY)
-    mass, weighted = lax.psum((local_mass, slice_sum), "seq")
+    mass, weighted = seq_psum((local_mass, slice_sum))
     collected_rows = weighted / mass[..., None]
     token_mixer = jnp.einsum(
         "svy,syc->svc", inverse_rounds(anchor_block), collected_rows, precision=HIGH_ACCURACY
@@ -75,7 +103,7 @@
         .reshape(tok, width)
         .astype(jnp.bfloat16)
     )
-    full_out = lax.all_gather(w_out, "seq", axis=1, tiled=True)
+    full_out = seq_gather(w_out, 1)
     out_terms = jnp.dot(attn, full_out, preferred_element_type=jnp.float32)
     proj = lax.psum_scatter(
         out_terms.astype(jnp.bfloat16), "mp", scatter_dimension=1, tiled=True
@@ -86,13 +114,13 @@
     meansq = jnp.mean(whole32 * whole32, axis=-1, keepdims=True)
     normed = (whole32 * lax.rsqrt(meansq + EPS) * gain[None, :]).astype(jnp.bfloat16)
     full_gate, full_up = (
-        lax.all_gather(w_gate, "seq", axis=0, tiled=True),
-        lax.all_gather(w_up, "seq", axis=0, tiled=True),
+        seq_gather(w_gate, 0),
+        seq_gather(w_up, 0),
     )
     gate = jnp.dot(normed, full_gate, preferred_element_type=jnp.float32)
     upper = jnp.dot(normed, full_up, preferred_element_type=jnp.float32)
     hidden = (jax.nn.silu(gate) * upper).astype(jnp.bfloat16)
-    full_down = lax.all_gather(w_down, "seq", axis=1, tiled=True)
+    full_down = seq_gather(w_down, 1)
     down_terms = jnp.dot(hidden, full_down, preferred_element_type=jnp.float32)
     ffn = lax.psum_scatter(
         down_terms.astype(jnp.bfloat16), "mp", scatter_dimension=1, tiled=True
@@ -100,22 +128,31 @@
     return (resid.astype(jnp.float32) + ffn).astype(jnp.bfloat16)
 
 
+def split_mesh(mesh):
+    n_seq = mesh.shape["seq"]
+    n_mp = mesh.shape["mp"]
+    devs = mesh.devices.reshape(n_seq // 8, 4, 2, n_mp)
+    return Mesh(devs, SEQ_AXES + ("mp",))
+
+
 def solution(mesh):
+    fine = split_mesh(mesh)
+    S = SEQ_AXES
     return jax.shard_map(
         on_device,
-        mesh=mesh,
+        mesh=fine,
         in_specs=(
-            P("seq", "mp"),
-            P("seq", "mp"),
-            P("seq", "mp"),
-            P("seq", "mp"),
+            P(S, "mp"),
+            P(S, "mp"),
+            P(S, "mp"),
+            P(S, "mp"),
             P(),
             P(),
-            P("mp", "seq"),
-            P("seq", "mp"),
-            P("seq", "mp"),
-            P("mp", "seq"),
+            P("mp", S),
+            P(S, "mp"),
+            P(S, "mp"),
+            P("mp", S),
         ),
-        out_specs=P("seq", "mp"),
+        out_specs=P(S, "mp"),
         check_vma=False,
     )

time: 1540 us -> 899 us (0.58)
  blocking collectives: 494 us -> 153 us
  waiting for transfers between devices: 999 us -> 698 us
    all_gather x4, waiting for transfers between devices: 537 us -> 254 us  [seq_gather(): x = lax.all_gather(x, ax, axis=axis, tiled=True)]
    psum x1 -> x3, blocking collectives: 247 us -> 41.9 us  [seq_psum(): x = lax.psum(x, ax)]
    pmax x1 -> x3, blocking collectives: 234 us -> 39.4 us  [seq_pmax(): x = lax.pmax(x, ax)]
    all_gather x0 -> x8, blocking collectives: none -> 59.2 us  [seq_gather(): x = lax.all_gather(x, ax, axis=axis, tiled=True)]
    reduce_scatter x1, waiting for transfers between devices: 23.7 us -> 0.02 us  [on_device(): lax.psum_scatter(out_terms.astype(jnp.bfloat16), 'mp', scatter_dimension=...]
    psum x2 -> x6, waiting for transfers between devices: 410 us -> 419 us  [seq_psum(): x = lax.psum(x, ax)]
  transfers between devices with their start and end apart: 8 -> 12, of which waited for: 8 -> 11; matrix products, arithmetic and copies ran while one was open for 1% -> 2% of each run, Pallas kernels for 0% -> 0%
where the time goes in v1:
time: 899 us; the launch traced here: 898 us
  waiting for transfers between devices  698 us (78%)
  blocking collectives  153 us (17%)
  matrix products  27.2 us (3%)
  between operations  13.9 us (2%)
    psum x6, waiting for transfers between devices, seq_psum(): x = lax.psum(x, ax)  419 us
    all_gather x4, waiting for transfers between devices, seq_gather(): x = lax.all_gather(x, ax, axis=axis, tiled=True)  254 us
    all_gather x8, blocking collectives, seq_gather(): x = lax.all_gather(x, ax, axis=axis, tiled=True)  59.2 us
    psum x3, blocking collectives, seq_psum(): x = lax.psum(x, ax)  41.9 us
    pmax x3, blocking collectives, seq_pmax(): x = lax.pmax(x, ax)  39.4 us
    reduce_scatter x1, waiting for transfers between devices, on_device(): lax.psum_scatter(down_terms.astype(jnp.bfloat16), 'mp', scatter_dimension...  25.5 us
  transfers between devices with their start and end apart: 12, of which 11 were waited for; matrix products, arithmetic and copies ran while one was open for 2% of the time, Pallas kernels for 0%

profile of v1, /device:TPU:24, one launch (start us, length us, event | category | flops | bytes accessed | tf_op | source)
XLA Modules:
  0.0 897.7 jit_solution(6674127213677721697)
XLA Ops:
  6.5 0.8 copy.40
  7.5 0.7 fusion.82
  8.3 1.8 fusion.60
  10.1 43.3 %all-reduce.10.cloned.1.call-done = f32[64,512]{1,0:T(8,128)} async-done(((f32[64,512]{1,0:T(8,128)}), f32[64,512]{1,0:T(8,128)}) %all-reduce.10.cloned.1.call-update) | async-done | bytes 131088 | tf_op jit(solution)/shard_map/psum | solution.py:35
  53.5 59.0 %all-reduce.12.cloned.1.call-done = f32[64,512]{1,0:T(8,128)} async-done(((f32[64,512]{1,0:T(8,128)}), f32[64,512]{1,0:T(8,128)}) %all-reduce.12.cloned.1.call-update) | async-done | bytes 131088 | tf_op jit(solution)/shard_map/psum | solution.py:35
  112.6 0.9 fusion.59
  113.6 137.6 %all-reduce.14.cloned.1.call-done = f32[64,512]{1,0:T(8,128)} async-done(((f32[64,512]{1,0:T(8,128)}), f32[64,512]{1,0:T(8,128)}) %all-reduce.14.cloned.1.call-update) | async-done | bytes 131088 | tf_op jit(solution)/shard_map/psum | solution.py:35
  251.1 1.2 fusion.83
  252.4 2.5 pmax.21
  254.9 7.4 pmax.22
  262.3 29.5 %pmax.23 = f32[4,64]{1,0:T(4,128)S(1)} all-reduce(f32[4,64]{1,0:T(4,128)S(1)} %pmax.22), channel_id=1, replica_groups=mesh['z'=16,'y'=4,'c'=2,'mp'=4] {'z'}, use_global_device_ids=true, to_apply=%region_16.17 | all-reduce | flops 256 | bytes 2048 | tf_op jit(solution)/shard_map/pmax | solution.py:41
  291.8 1.8 fusion.29
  293.6 36.2 %all-reduce.20.cloned.1.call-done = (f32[64,512]{1,0:T(8,128)}, f32[4,64,128]{2,1,0:T(8,128)}) async-done(((f32[64,512]{1,0:T(8,128)}, f32[4,64,128]{2,1,0:T(8,128)}), (f32[64,512]{1,0:T(8,128)}, f32[4,64,128]{2,1,0:T(8,128)})) %all-reduce.20.cloned.1.call-update) | async-done | bytes 262160 | tf_op jit(solution)/shard_map/psum | solution.py:35
  329.9 59.7 %all-reduce.18.cloned.1.call-done = (f32[64,512]{1,0:T(8,128)}, f32[4,64,128]{2,1,0:T(8,128)}) async-done(((f32[64,512]{1,0:T(8,128)}, f32[4,64,128]{2,1,0:T(8,128)}), (f32[64,512]{1,0:T(8,128)}, f32[4,64,128]{2,1,0:T(8,128)})) %all-reduce.18.cloned.1.call-update) | async-done | bytes 262160 | tf_op jit(solution)/shard_map/psum | solution.py:35
  389.7 2.0 all_gather.39
  391.7 12.7 %all_gather.40 = bf16[512,128]{0,1:T(8,128)(2,1)} all-gather(bf16[512,32]{0,1:T(8,128)(2,1)S(1)} %all_gather.39), channel_id=1, replica_groups=mesh['z'=16,'y'=4,'c'=2,'mp'=4] {'y'}, dimensions={1}, use_global_device_ids=true | all-gather | bytes 163840 | tf_op jit(solution)/shard_map/all_gather | solution.py:47
  404.6 2.5 psum.93
  407.1 8.1 psum.94
  415.2 31.3 %psum.95 = f32[4,64]{1,0:T(4,128)S(1)} all-reduce(f32[4,64]{1,0:T(4,128)S(1)} %psum.94), channel_id=1, replica_groups=mesh['z'=16,'y'=4,'c'=2,'mp'=4] {'z'}, use_global_device_ids=true, to_apply=%region_23.24 | all-reduce | flops 256 | bytes 2048 | tf_op jit(solution)/shard_map/psum | solution.py:35
  446.5 82.6 %all-reduce.16.cloned.1.call-done = (f32[64,512]{1,0:T(8,128)}, f32[4,64,128]{2,1,0:T(8,128)}) async-done(((f32[64,512]{1,0:T(8,128)}, f32[4,64,128]{2,1,0:T(8,128)}), (f32[64,512]{1,0:T(8,128)}, f32[4,64,128]{2,1,0:T(8,128)})) %all-reduce.16.cloned.1.call-update) | async-done | bytes 262160 | tf_op jit(solution)/shard_map/psum | solution.py:35
  529.2 1.3 fusion.85
  530.5 1.4 fusion.84
  532.3 0.4 fusion.68
  532.8 0.3 convolution_subtract_fusion.11
  533.0 0.3 convolution_subtract_fusion.10
  533.3 0.3 convolution_multiply_fusion.8
  533.6 0.4 fusion.77
  534.0 0.3 convolution_subtract_fusion.9
  534.3 0.3 convolution_subtract_fusion.8
  534.6 0.3 convolution_multiply_fusion.7
  534.8 0.4 fusion.75
  535.4 0.3 convolution_subtract_fusion.7
  535.7 0.3 convolution_subtract_fusion.6
  536.0 0.3 convolution_multiply_fusion.6
  536.2 0.4 fusion.73
  536.6 0.3 convolution_subtract_fusion.5
  536.9 0.3 convolution_subtract_fusion.4
  537.2 0.3 convolution_multiply_fusion.5
  537.4 0.4 fusion.71
  537.8 0.3 convolution_subtract_fusion.3
  538.1 0.3 convolution_subtract_fusion.2
  538.4 0.3 convolution_multiply_fusion.4
  538.6 0.4 fusion.69
  539.1 0.3 convolution_subtract_fusion.1
  539.6 0.3 convolution_multiply_fusion.3
  539.9 0.4 fusion.22
  540.2 0.4 fusion.2
  540.6 60.8 %all-gather.5.cloned.1.call-done = bf16[512,2048]{0,1:T(8,128)(2,1)} async-done(((bf16[512,128]{0,1:T(8,128)(2,1)}), bf16[512,2048]{0,1:T(8,128)(2,1)}) %all-gather.5.cloned.1.call-update) | async-done | bytes 2097168 | tf_op jit(solution)/shard_map/all_gather | solution.py:47
  601.4 3.0 convolution_convert_fusion.1
  604.6 1.8 all_gather.43
  606.4 12.9 %all_gather.44 = bf16[128,768]{1,0:T(8,128)(2,1)} all-gather(bf16[32,768]{1,0:T(8,128)(2,1)S(1)} %all_gather.43), channel_id=1, replica_groups=mesh['z'=16,'y'=4,'c'=2,'mp'=4] {'y'}, dimensions={0}, use_global_device_ids=true | all-gather | bytes 245760 | tf_op jit(solution)/shard_map/all_gather | solution.py:47
  619.4 1.8 all_gather.49
  621.2 13.0 %all_gather.50 = bf16[768,128]{0,1:T(8,128)(2,1)} all-gather(bf16[768,32]{0,1:T(8,128)(2,1)S(1)} %all_gather.49), channel_id=1, replica_groups=mesh['z'=16,'y'=4,'c'=2,'mp'=4] {'y'}, dimensions={1}, use_global_device_ids=true | all-gather | bytes 245760 | tf_op jit(solution)/shard_map/all_gather | solution.py:47
  634.3 1.8 all_gather.46
  636.1 13.1 %all_gather.47 = bf16[128,768]{1,0:T(8,128)(2,1)} all-gather(bf16[32,768]{1,0:T(8,128)(2,1)S(1)} %all_gather.46), channel_id=1, replica_groups=mesh['z'=16,'y'=4,'c'=2,'mp'=4] {'y'}, dimensions={0}, use_global_device_ids=true | all-gather | bytes 245760 | tf_op jit(solution)/shard_map/all_gather | solution.py:47
  649.3 0.9 add_convert_fusion.1
  650.1 12.6 %all_gather.42 = bf16[64,2048]{1,0:T(8,128)(2,1)S(1)} all-gather(bf16[64,512]{1,0:T(8,128)(2,1)S(1)} %add_convert_fusion.1), channel_id=1, replica_groups=mesh['z'=16,'y'=4,'c'=2,'mp'=4] {'mp'}, dimensions={1}, use_global_device_ids=true | all-gather | bytes 327680 | tf_op jit(solution)/shard_map/all_gather | solution.py:112
  662.9 45.1 %all-gather.7.cloned.1.call-done = bf16[2048,768]{1,0:T(8,128)(2,1)} async-done(((bf16[128,768]{1,0:T(8,128)(2,1)}), bf16[2048,768]{1,0:T(8,128)(2,1)}) %all-gather.7.cloned.1.call-update) | async-done | bytes 3145744 | tf_op jit(solution)/shard_map/all_gather | solution.py:47
  708.0 2.6 fusion.36
  710.6 72.6 %all-gather.11.cloned.1.call-done = bf16[768,2048]{0,1:T(8,128)(2,1)} async-done(((bf16[768,128]{0,1:T(8,128)(2,1)}), bf16[768,2048]{0,1:T(8,128)(2,1)}) %all-gather.11.cloned.1.call-update) | async-done | bytes 3145744 | tf_op jit(solution)/shard_map/all_gather | solution.py:47
  783.2 75.4 %all-gather.9.cloned.1.call-done = bf16[2048,768]{1,0:T(8,128)(2,1)} async-done(((bf16[128,768]{1,0:T(8,128)(2,1)}), bf16[2048,768]{1,0:T(8,128)(2,1)}) %all-gather.9.cloned.1.call-update) | async-done | bytes 3145744 | tf_op jit(solution)/shard_map/all_gather | solution.py:47
  858.5 5.3 convolution_convert_fusion
  863.9 25.5 %reduce-scatter.5.cloned.1.call-done = bf16[64,512]{1,0:T(8,128)(2,1)} async-done(((bf16[64,2048]{1,0:T(8,128)(2,1)}), bf16[64,512]{1,0:T(8,128)(2,1)}) %reduce-scatter.5.cloned.1.call-update) | async-done | bytes 65552 | tf_op jit(solution)/shard_map/reduce_scatter | solution.py:125
  889.4 1.5 add_convert_fusion
  (55 shorter events, 2.0 us)
Async XLA Ops:
  6.5 106.1 %copy-start = (bf16[64,512]{1,0:T(8,128)(2,1)S(1)}, bf16[64,512]{1,0:T(8,128)(2,1)}, u32[]{:S(2)}) copy-start(bf16[64,512]{1,0:T(8,128)(2,1)} %param.11) | copy-start | bytes 196612
  6.5 522.6 %copy-start.1 = (bf16[64,512]{1,0:T(8,128)(2,1)S(1)}, bf16[64,512]{1,0:T(8,128)(2,1)}, u32[]{:S(2)}) copy-start(bf16[64,512]{1,0:T(8,128)(2,1)} %param.10) | copy-start | bytes 196612
  6.5 46.9 %all-reduce.10.cloned.1.call-start = ((), (), s32[]{:S(2)}) async-start(), calls=%async_computation.2 | async-start | bytes 262144 | tf_op jit(solution)/shard_map/psum | solution.py:35
  10.1 102.5 %all-reduce.12.cloned.1.call-start = ((), (), s32[]{:S(2)}) async-start(), calls=%async_computation.3 | async-start | bytes 262144 | tf_op jit(solution)/shard_map/psum | solution.py:35
  53.5 197.7 %all-reduce.14.cloned.1.call-start = ((), (), s32[]{:S(2)}) async-start(), calls=%async_computation.4 | async-start | bytes 262144 | tf_op jit(solution)/shard_map/psum | solution.py:35
  112.6 217.2 %all-reduce.20.cloned.1.call-start = ((), (), s32[]{:S(2)}) async-start(), calls=%async_computation.13 | async-start | bytes 524288 | tf_op jit(solution)/shard_map/psum | solution.py:35
  293.6 96.0 %all-reduce.18.cloned.1.call-start = ((), (), s32[]{:S(2)}) async-start(), calls=%async_computation.12 | async-start | bytes 524288 | tf_op jit(solution)/shard_map/psum | solution.py:35
  329.9 199.3 %all-reduce.16.cloned.1.call-start = ((), (), s32[]{:S(2)}) async-start(), calls=%async_computation.11 | async-start | bytes 524288 | tf_op jit(solution)/shard_map/psum | solution.py:35
  389.7 211.8 %all-gather.5.cloned.1.call-start = ((), (), s32[]{:S(2)}) async-start(), calls=%async_computation.5 | async-start | bytes 2228224 | tf_op jit(solution)/shard_map/all_gather | solution.py:47
  404.5 244.8 %reduce-scatter.3.cloned.1.call-start = ((), (), s32[]{:S(2)}) async-start(), calls=%async_computation.6 | async-start | bytes 327680 | tf_op jit(solution)/shard_map/reduce_scatter | solution.py:108
  535.7 4.2 copy-start.7
  538.1 66.5 %copy-start.4 = (bf16[16,768]{1,0:T(8,128)(2,1)S(1)}, bf16[16,768]{1,0:T(8,128)(2,1)}, u32[]{:S(2)}) copy-start(bf16[16,768]{1,0:T(8,128)(2,1)} %param.17) | copy-start | bytes 73732
  538.4 81.0 %copy-start.5 = (bf16[768,16]{0,1:T(8,128)(2,1)S(1)}, bf16[768,16]{0,1:T(8,128)(2,1)}, u32[]{:S(2)}) copy-start(bf16[768,16]{0,1:T(8,128)(2,1)} %param.19) | copy-start | bytes 73732
  539.0 95.2 %copy-start.6 = (bf16[16,768]{1,0:T(8,128)(2,1)S(1)}, bf16[16,768]{1,0:T(8,128)(2,1)}, u32[]{:S(2)}) copy-start(bf16[16,768]{1,0:T(8,128)(2,1)} %param.18) | copy-start | bytes 73732
  539.3 109.9 %copy-start.2 = (bf16[64,512]{1,0:T(8,128)(2,1)S(1)}, bf16[64,512]{1,0:T(8,128)(2,1)}, u32[]{:S(2)}) copy-start(bf16[64,512]{1,0:T(8,128)(2,1)} %param.13) | copy-start | bytes 196612
  539.6 168.4 %copy-start.3 = (f32[2048]{0:T(1024)S(1)}, f32[2048]{0:T(1024)}, u32[]{:S(2)}) copy-start(f32[2048]{0:T(1024)} %param.15) | copy-start | bytes 24580
  604.5 103.4 %all-gather.7.cloned.1.call-start = ((), (), s32[]{:S(2)}) async-start(), calls=%async_computation.7 | async-start | bytes 3342336 | tf_op jit(solution)/shard_map/all_gather | solution.py:47
  619.3 163.8 %all-gather.11.cloned.1.call-start = ((), (), s32[]{:S(2)}) async-start(), calls=%async_computation.9 | async-start | bytes 3342336 | tf_op jit(solution)/shard_map/all_gather | solution.py:47
  634.2 224.3 %all-gather.9.cloned.1.call-start = ((), (), s32[]{:S(2)}) async-start(), calls=%async_computation.8 | async-start | bytes 3342336 | tf_op jit(solution)/shard_map/all_gather | solution.py:47
  649.2 240.2 %reduce-scatter.5.cloned.1.call-start = ((), (), s32[]{:S(2)}) async-start(), calls=%async_computation.10 | async-start | bytes 327680 | tf_op jit(solution)/shard_map/reduce_scatter | solution.py:125
Sparse Core Ops, SparseCore 0:
  10.2 43.1 all-reduce.9
  55.7 56.7 all-reduce.11
  115.0 136.1 all-reduce.13
  293.7 36.0 all-reduce.19
  332.2 57.3 all-reduce.17
  391.8 137.2 all-reduce.15
  531.5 69.9 all-gather.4
  604.6 25.1 reduce-scatter.2
  631.9 75.9 all-gather.6
  709.9 73.2 all-gather.10
  785.2 73.2 all-gather.8
  864.0 25.3 reduce-scatter.4
